TPU v7x, 256 devices: a whole 4x4x8 slice. The times are simulated.
256 devices in a mesh: dp: 4 (over x), rows: 64 (over y, z, core).
Axes of the slice: x: 4, y: 4, z: 8, core: 2. Of those that a mesh axis runs over, the one named last changes fastest.
Arguments:
- grads: bfloat16 [4, 64, 1024, 1024], P('dp', None, 'rows'), may hold values from -6 to 6
- weight: bfloat16 [64, 1024, 1024], P(None, 'rows'), may hold values from -6 to 6
- basis: float32 [64, 1024, 256], P(None, 'rows'), may hold values from -6 to 6
- first_moment: float32 [256, 256, 1024], P('rows', None, 'dp'), may hold values from -6 to 6
- second_moment: float32 [256, 256, 1024], P('rows', None, 'dp'), may hold values from 0.5 to 4
- sketch: bfloat16 [1024, 256], replicated, may hold values from -6 to 6
- owner: int32 [64], replicated, may hold values from 0 to 63, as said below
- rank: int32 [64], replicated, may hold values from 128 to 256
Outputs:
- new_weight: bfloat16 [64, 1024, 1024], P(None, 'rows')
- new_basis: float32 [64, 1024, 256], P(None, 'rows')
- first_out: float32 [256, 256, 1024], P('rows', None, 'dp')
- second_out: float32 [256, 256, 1024], P('rows', None, 'dp')
Inputs may be any that keep to these rules, and one draw needn't show every extreme that they name: No owner is named by more than 4 matrices, and some owner is named by exactly 4.
All inputs are finite; a program needn't handle non-finite values.
Results may differ from a plain program's by a relative error of at most 0.012.
Values may be sent and summed in bfloat16 or wider, within the bound.
A program may use at most 128 MiB of HBM per device.

v0:
```python
import jax
import jax.numpy as jnp
from jax import lax
from jax.sharding import PartitionSpec as P

beta_one = 0.9
beta_two = 0.95
bias_one = 1.0 - 0.9**10
bias_two = 1.0 - 0.95**10
step_size = 0.5
epsilon = 1e-08


def slot_of(owner, capacity):
    same = owner[:, None] == owner[None, :]
    places = jnp.arange(owner.shape[0], dtype=jnp.int32)
    earlier = places[None, :] < places[:, None]
    within = jnp.sum((same & earlier).astype(jnp.int32), axis=1)
    return owner * capacity + within


def spread_half(placing, data, capacity, owners):
    flat = data.reshape(data.shape[0], -1)
    moved = jnp.dot(placing.T, flat, preferred_element_type=jnp.float32).astype(jnp.bfloat16)
    return moved.reshape(capacity, owners, data.shape[1], data.shape[2])


def spread_full(placing, data, capacity, owners):
    flat = data.reshape(data.shape[0], -1)
    moved = jnp.dot(placing.T, flat, precision=lax.Precision.HIGHEST)
    return moved.reshape(capacity, owners, data.shape[1], data.shape[2])


def collect_half(placing, data):
    flat = data.reshape(placing.shape[1], -1)
    picked = jnp.dot(placing, flat, preferred_element_type=jnp.float32).astype(jnp.bfloat16)
    return picked.reshape(placing.shape[0], data.shape[2], data.shape[3])


def collect_full(placing, data):
    flat = data.reshape(placing.shape[1], -1)
    picked = jnp.dot(placing, flat, precision=lax.Precision.HIGHEST)
    return picked.reshape(placing.shape[0], data.shape[2], data.shape[3])


def per_device(grads, weight, basis, first_moment, second_moment, sketch, owner, rank):
    owners = lax.axis_size("rows")
    here = lax.axis_index("rows")
    group = lax.axis_index("dp")
    capacity = first_moment.shape[0]
    rank_full = first_moment.shape[1]
    quarter = first_moment.shape[2]
    shard = weight.shape[1]
    width = weight.shape[2]
    total_rows = shard * owners
    root = float(total_rows) ** 0.5
    inverse_root = float(total_rows) ** (-0.5)
    slots = slot_of(owner, capacity)
    column = slots % capacity * owners + slots // capacity
    placing = column[:, None] == jnp.arange(capacity * owners, dtype=jnp.int32)[None, :]
    place_half = placing.astype(jnp.bfloat16)
    place_full = placing.astype(jnp.float32)
    sent_basis = lax.all_to_all(
        spread_full(place_full, basis, capacity, owners),
        "rows",
        split_axis=1,
        concat_axis=1,
        tiled=True,
    )
    old_basis = sent_basis.reshape(capacity, total_rows, rank_full)
    total = lax.psum(grads[0], "dp").astype(jnp.float32).astype(jnp.bfloat16)
    sent_grad = lax.all_to_all(
        spread_half(place_half, total, capacity, owners),
        "rows",
        split_axis=1,
        concat_axis=1,
        tiled=True,
    )
    whole = sent_grad.reshape(capacity, total_rows, width)
    own = lax.dynamic_slice_in_dim(whole, group * quarter, quarter, 2)
    sample = jnp.einsum("cmd,dr->cmr", whole, sketch, preferred_element_type=jnp.float32)
    matched = slots[:, None] == (here * capacity + jnp.arange(capacity, dtype=jnp.int32))[None, :]
    valid = jnp.any(matched, axis=0).astype(jnp.float32)
    rank_slot = jnp.sum(jnp.where(matched, rank[:, None], 0), axis=0)
    projected = (
        jnp.einsum(
            "cmr,cmd->crd", old_basis, own.astype(jnp.float32), precision=lax.Precision.HIGHEST
        )
        * inverse_root
    )
    first_new = beta_one * first_moment + (1.0 - beta_one) * projected
    second_new = beta_two * second_moment + (1.0 - beta_two) * projected * projected
    keeping = (jnp.arange(rank_full, dtype=jnp.int32)[None, :] < rank_slot[:, None]).astype(
        jnp.float32
    )[:, :, None]
    update = keeping * (first_new / bias_one) / (jnp.sqrt(second_new / bias_two) + epsilon)
    delta = (
        jnp.einsum("cmr,crd->cmd", old_basis, update, precision=lax.Precision.HIGHEST)
        * inverse_root
    ).astype(jnp.bfloat16)
    gram = jnp.einsum("cmr,cms->crs", sample, sample, precision=lax.Precision.HIGHEST)
    gram = gram + (1.0 - valid)[:, None, None] * jnp.eye(rank_full, dtype=jnp.float32)[None, :, :]
    lower = jnp.linalg.cholesky(gram)
    new_basis = (
        lax.linalg.triangular_solve(lower, sample, left_side=False, lower=True, transpose_a=True)
        * root
    )
    back_delta = lax.all_to_all(
        delta.reshape(capacity, owners, shard, quarter),
        "rows",
        split_axis=1,
        concat_axis=1,
        tiled=True,
    )
    full_delta = lax.all_gather(collect_half(place_half, back_delta), "dp", axis=2, tiled=True)
    back_basis = lax.all_to_all(
        new_basis.reshape(capacity, owners, shard, rank_full),
        "rows",
        split_axis=1,
        concat_axis=1,
        tiled=True,
    )
    mine_basis = collect_full(place_full, back_basis)
    new_weight = (weight.astype(jnp.float32) - step_size * full_delta.astype(jnp.float32)).astype(
        jnp.bfloat16
    )
    scale_slot = valid[:, None, None]
    return (new_weight, mine_basis, first_new * scale_slot, second_new * scale_slot)


def solution(mesh):
    in_specs = (
        P("dp", None, "rows", None),
        P(None, "rows", None),
        P(None, "rows", None),
        P("rows", None, "dp"),
        P("rows", None, "dp"),
        P(),
        P(),
        P(),
    )
    out_specs = (
        P(None, "rows", None),
        P(None, "rows", None),
        P("rows", None, "dp"),
        P("rows", None, "dp"),
    )
    return jax.shard_map(
        per_device, mesh=mesh, in_specs=in_specs, out_specs=out_specs, check_vma=False
    )
```

profile of v0, /device:TPU:1, one launch (start us, length us, event | category | flops | bytes accessed | tf_op | source)
XLA Modules:
  0.0 740.5 jit_solution(191552147987780826)
XLA Ops:
  7.2 0.9 convert_reduce_fusion
  8.1 0.7 fusion.41
  8.8 3.5 fusion.5
  12.3 4.4 copy.72
  16.7 13.5 %all-to-all-start = ((f32[4,64,16,256]{3,2,0,1:T(8,128)}), f32[4,64,16,256]{3,2,0,1:T(8,128)}, u32[]{:S(2)}, u32[]{:S(2)}) async-start(f32[4,64,16,256]{3,2,0,1:T(8,128)} %copy.72), calls=%async_computation | async-start | bytes 8388608 | tf_op jit(solution)/shard_map/all_to_all | solution.py:63
  30.4 2.6 copy.105
  33.1 65.7 %all-reduce.3.cloned.1.call-done = bf16[64,16384]{1,0:T(8,128)(2,1)} async-done(((bf16[64,16384]{1,0:T(8,128)(2,1)}), bf16[64,16384]{1,0:T(8,128)(2,1)}) %all-reduce.3.cloned.1.call-update) | async-done | bytes 2097168 | tf_op jit(solution)/shard_map/psum | solution.py:71
  98.7 7.3 convolution_convert_fusion
  106.0 15.6 %copy.106 = bf16[32,8,16,1024]{3,2,1,0:T(8,128)(2,1)} copy(bf16[32,8,16,1024]{3,1,2,0:T(8,128)(2,1)} %bitcast.92) | data formatting | bytes 16777216
  121.6 8.5 %copy.74 = bf16[4,64,16,1024]{3,2,0,1:T(8,128)(2,1)} copy(bf16[4,64,16,1024]{3,2,1,0:T(8,128)(2,1)} %bitcast.93) | data formatting | bytes 16777216 | tf_op jit(solution)/shard_map/reshape | solution.py:25
  130.2 11.0 %all-to-all-start.1 = ((bf16[4,64,16,1024]{3,2,0,1:T(8,128)(2,1)}), bf16[4,64,16,1024]{3,2,0,1:T(8,128)(2,1)}, u32[]{:S(2)}, u32[]{:S(2)}) async-start(bf16[4,64,16,1024]{3,2,0,1:T(8,128)(2,1)} %copy.74), calls=%async_computation.1 | async-start | bytes 16777216 | tf_op jit(solution)/shard_map/all_to_all | solution.py:72
  141.8 4.8 copy.73
  146.6 180.4 %all-to-all-done.1 = bf16[4,64,16,1024]{3,2,0,1:T(8,128)(2,1)} async-done(((bf16[4,64,16,1024]{3,2,0,1:T(8,128)(2,1)}), bf16[4,64,16,1024]{3,2,0,1:T(8,128)(2,1)}, u32[]{:S(2)}, u32[]{:S(2)}) %all-to-all-start.1) | async-done | bytes 8388640 | tf_op jit(solution)/shard_map/all_to_all | solution.py:72
  327.0 8.5 %copy.75 = bf16[4,64,16,1024]{3,2,1,0:T(8,128)(2,1)} copy(bf16[4,64,16,1024]{3,2,0,1:T(8,128)(2,1)} %all-to-all-done.1) | data formatting | bytes 16777216 | tf_op jit(solution)/shard_map/all_to_all | solution.py:72
  335.5 7.8 %fusion.14 = f32[4,1024,256]{2,1,0:T(8,128)} fusion(bf16[4,1024,1024]{2,1,0:T(8,128)(2,1)} %bitcast.100, bf16[1024,256]{1,0:T(8,128)(2,1)S(1)} %copy-done), kind=kOutput, calls=%fused_computation.29 | convolution fusion | flops 2147483648 | bytes 13107200 | tf_op jit(solution)/shard_map/cmd,dr->cmr/dot_general | solution.py:81
  343.4 6.8 broadcast_multiply_fusion
  350.2 4.7 multiply_convert_fusion
  354.9 1.6 copy.77
  356.6 6.4 all-to-all-start.2
  363.0 10.0 %fusion.50 = f32[4,256,256]{2,1,0:T(8,128)S(1)} fusion(f32[4,1024,256]{2,1,0:T(8,128)} %fusion.14), kind=kOutput, calls=%fused_computation.97 | convolution fusion | flops 3221225472 | bytes 5242880 | tf_op jit(solution)/shard_map/cmr,cms->crs/dot_general | solution.py:101
  373.6 1.0 copy-done.4
  374.6 46.9 %custom-call.16 = f32[4,128,128]{2,1,0:T(8,128)S(1)} custom-call(f32[4,128,128]{2,1,0:T(8,128)S(1)} %cholesky.122), custom_call_target="Cholesky" | custom-call | tf_op jit(solution)/shard_map/jit(cholesky)/cholesky | solution.py:103
  421.7 39.3 %custom-call.17 = f32[4,1,128,128]{2,3,1,0:T(8,128)S(1)} custom-call(f32[4,1,128,128]{3,2,1,0:T(8,128)S(1)} %select_bitcast_fusion), custom_call_target="InvertDiagBlocksLowerTriangular" | custom-call | tf_op jit(solution)/shard_map/jit(cholesky)/cholesky | solution.py:103
  461.0 1.4 constant_dynamic-update-slice_fusion.1
  462.3 1.6 convolution_subtract_fusion
  464.0 47.1 %custom-call.18 = f32[4,128,128]{2,1,0:T(8,128)S(1)} custom-call(f32[4,128,128]{2,1,0:T(8,128)S(1)} %convolution_subtract_fusion), custom_call_target="Cholesky" | custom-call | tf_op jit(solution)/shard_map/jit(cholesky)/cholesky | solution.py:103
  511.7 5.3 while.1
  511.7 0.6 fusion.63
  512.3 2.1 bitcast_dynamic-update-slice_fusion.2
  514.3 0.6 fusion.63
  514.9 2.1 bitcast_dynamic-update-slice_fusion.2
  517.0 79.4 %custom-call.19 = f32[4,2,128,128]{2,3,1,0:T(8,128)S(1)} custom-call(f32[4,2,128,128]{3,2,1,0:T(8,128)} %bitcast.111), custom_call_target="InvertDiagBlocksLowerTriangular" | custom-call | tf_op jit(solution)/shard_map/triangular_solve | solution.py:105
  596.4 3.7 fusion.1
  600.1 1.9 fusion.19
  602.1 2.0 fusion
  604.1 2.5 copy_multiply_fusion
  606.5 10.5 %all-to-all-start.3 = ((f32[4,64,16,256]{3,2,0,1:T(8,128)}), f32[4,64,16,256]{3,2,0,1:T(8,128)}, u32[]{:S(2)}, u32[]{:S(2)}) async-start(f32[4,64,16,256]{3,2,0,1:T(8,128)} %copy_multiply_fusion), calls=%async_computation.3 | async-start | bytes 8388608 | tf_op jit(solution)/shard_map/all_to_all | solution.py:116
  617.4 1.8 copy.78
  619.2 0.9 copy.107
  620.6 0.9 copy.108
  621.6 35.8 %all-gather.2.cloned.1.call-done = bf16[64,16,1024]{2,1,0:T(8,128)(2,1)} async-done(((bf16[64,16,256]{2,1,0:T(8,128)(2,1)}), bf16[64,16,1024]{2,1,0:T(8,128)(2,1)}) %all-gather.2.cloned.1.call-update) | async-done | bytes 2097168 | tf_op jit(solution)/shard_map/all_gather | solution.py:115
  657.3 3.9 subtract_convert_fusion
  661.2 51.7 %all-to-all-done.3 = f32[4,64,16,256]{3,2,0,1:T(8,128)} async-done(((f32[4,64,16,256]{3,2,0,1:T(8,128)}), f32[4,64,16,256]{3,2,0,1:T(8,128)}, u32[]{:S(2)}, u32[]{:S(2)}) %all-to-all-start.3) | async-done | bytes 4194336 | tf_op jit(solution)/shard_map/all_to_all | solution.py:116
  712.9 2.8 copy.88
  715.7 5.7 copy.109
  721.5 5.7 copy.89
  727.1 4.5 fusion.31
  731.6 1.6 copy.90
  (52 shorter events, 3.0 us)
Async XLA Ops:
  7.2 328.4 %copy-start = (bf16[1024,256]{1,0:T(8,128)(2,1)S(1)}, bf16[1024,256]{1,0:T(8,128)(2,1)}, u32[]{:S(2)}) copy-start(bf16[1024,256]{1,0:T(8,128)(2,1)} %param.13) | copy-start | bytes 1572868
  16.7 13.8 %copy-start.6 = (bf16[1,64,16,1024]{3,2,1,0:T(8,128)(2,1)S(1)}, bf16[1,64,16,1024]{3,2,1,0:T(8,128)(2,1)}, u32[]{:S(2)}) copy-start(bf16[1,64,16,1024]{3,2,1,0:T(8,128)(2,1)} %param.8) | copy-start | bytes 6291460
  16.7 113.5 %all-to-all-start = ((f32[4,64,16,256]{3,2,0,1:T(8,128)}), f32[4,64,16,256]{3,2,0,1:T(8,128)}, u32[]{:S(2)}, u32[]{:S(2)}) async-start(f32[4,64,16,256]{3,2,0,1:T(8,128)} %copy.72), calls=%async_computation | async-start | bytes 8388608 | tf_op jit(solution)/shard_map/all_to_all | solution.py:63
  30.2 68.6 %all-reduce.3.cloned.1.call-start = ((), (), s32[]{:S(2)}) async-start(), calls=%async_computation.4 | async-start | bytes 4194304 | tf_op jit(solution)/shard_map/psum | solution.py:71
  130.2 11.3 %copy-start.9 = (s32[64]{0:T(128)S(1)}, s32[64]{0:T(128)}, u32[]{:S(2)}) copy-start(s32[64]{0:T(128)} %param.15) | copy-start | bytes 772
  130.2 196.8 %all-to-all-start.1 = ((bf16[4,64,16,1024]{3,2,0,1:T(8,128)(2,1)}), bf16[4,64,16,1024]{3,2,0,1:T(8,128)(2,1)}, u32[]{:S(2)}, u32[]{:S(2)}) async-start(bf16[4,64,16,1024]{3,2,0,1:T(8,128)(2,1)} %copy.74), calls=%async_computation.1 | async-start | bytes 16777216 | tf_op jit(solution)/shard_map/all_to_all | solution.py:72
  335.5 7.9 %copy-start.3 = (f32[4,64,16,256]{3,2,1,0:T(8,128)S(1)}, f32[4,64,16,256]{3,2,1,0:T(8,128)}, u32[]{:S(2)}) copy-start(f32[4,64,16,256]{3,2,1,0:T(8,128)} %copy.73) | copy-start | bytes 12582916
  335.5 7.9 %copy-start.7 = (f32[4,256,256]{2,1,0:T(8,128)S(1)}, f32[4,256,256]{2,1,0:T(8,128)}, u32[]{:S(2)}) copy-start(f32[4,256,256]{2,1,0:T(8,128)} %param.12) | copy-start | bytes 3145732
  335.5 7.9 %copy-start.8 = (f32[4,256,256]{2,1,0:T(8,128)S(1)}, f32[4,256,256]{2,1,0:T(8,128)}, u32[]{:S(2)}) copy-start(f32[4,256,256]{2,1,0:T(8,128)} %param.11) | copy-start | bytes 3145732
  356.6 250.0 %all-to-all-start.2 = ((bf16[4,64,16,256]{3,2,0,1:T(8,128)(2,1)}), bf16[4,64,16,256]{3,2,0,1:T(8,128)(2,1)}, u32[]{:S(2)}, u32[]{:S(2)}) async-start(bf16[4,64,16,256]{3,2,0,1:T(8,128)(2,1)} %copy.77), calls=%async_computation.2 | async-start | bytes 4194304 | tf_op jit(solution)/shard_map/all_to_all | solution.py:108
  373.6 1.0 copy-start.4
  596.4 5.6 copy-start.2
  606.5 106.4 %all-to-all-start.3 = ((f32[4,64,16,256]{3,2,0,1:T(8,128)}), f32[4,64,16,256]{3,2,0,1:T(8,128)}, u32[]{:S(2)}, u32[]{:S(2)}) async-start(f32[4,64,16,256]{3,2,0,1:T(8,128)} %copy_multiply_fusion), calls=%async_computation.3 | async-start | bytes 8388608 | tf_op jit(solution)/shard_map/all_to_all | solution.py:116
  617.1 40.3 %all-gather.2.cloned.1.call-start = ((), (), s32[]{:S(2)}) async-start(), calls=%async_computation.5 | async-start | bytes 2621440 | tf_op jit(solution)/shard_map/all_gather | solution.py:115
  619.1 38.2 %copy-start.5 = (bf16[64,16,1024]{2,1,0:T(8,128)(2,1)S(1)}, bf16[64,16,1024]{2,1,0:T(8,128)(2,1)}, u32[]{:S(2)}) copy-start(bf16[64,16,1024]{2,1,0:T(8,128)(2,1)} %param.9) | copy-start | bytes 6291460
  721.5 11.7 %copy-start.1 = (bf16[1024,256]{1,0:T(8,128)(2,1)S(1)}, bf16[1024,256]{1,0:T(8,128)(2,1)}, u32[]{:S(2)}) copy-start(bf16[1024,256]{1,0:T(8,128)(2,1)} %param.13) | copy-start | bytes 1572868
Sparse Core Ops, SparseCore 0:
  33.9 64.7 all-reduce.2
  621.7 35.6 all-gather.1
where the time goes:
time: 746 us; the launch traced here: 740 us
  waiting for transfers between devices  334 us (45%)
  other arithmetic  222 us (30%)
  local copies, waits for them, and re-layouts  72.4 us (10%)
  matrix products  55.7 us (7%)
  starting transfers between devices  42 us (6%)
  between operations  14.8 us (2%)
    all_to_all x1, waiting for transfers between devices, per_device(): lax.all_to_all(spread_half(place_half, total, capacity, owners), 'rows',...  180 us
    another operation x10, other arithmetic, per_device(): lower = jnp.linalg.cholesky(gram)  134 us
    another operation x4, other arithmetic, per_device(): lax.linalg.triangular_solve(lower, sample, left_side=False, lower=True, t...  79.6 us
    psum x1, waiting for transfers between devices, per_device(): total = lax.psum(grads[0], 'dp').astype(jnp.float32).astype(jnp.bfloat16)  65.7 us
    all_to_all x1, waiting for transfers between devices, per_device(): lax.all_to_all(new_basis.reshape(capacity, owners, shard, rank_full), 'ro...  51.7 us
    all_gather x1, waiting for transfers between devices, per_device(): lax.all_gather(collect_half(place_half, back_delta), 'dp', axis=2, tiled=...  35.8 us
    unnamed x26, local copies, waits for them, and re-layouts  28.4 us
  transfers between devices with their start and end apart: 6, of which 4 were waited for; matrix products, arithmetic and copies ran while one was open for 39% of the time, Pallas kernels for 0%

commit v1 on v0

--- a/solution.py
+++ b/solution.py
@@ -113,12 +113,20 @@
         tiled=True,
     )
     full_delta = lax.all_gather(collect_half(place_half, back_delta), "dp", axis=2, tiled=True)
-    back_basis = lax.all_to_all(
-        new_basis.reshape(capacity, owners, shard, rank_full),
-        "rows",
-        split_axis=1,
-        concat_axis=1,
-        tiled=True,
+    back_basis = jnp.concatenate(
+        lax.all_to_all(
+            jnp.stack(
+                jnp.split(
+                    new_basis.reshape(capacity, owners, shard, rank_full),
+                    lax.axis_size("rows"),
+                    axis=1,
+                )
+            ),
+            "rows",
+            0,
+            0,
+        ),
+        axis=1,
     )
     mine_basis = collect_full(place_full, back_basis)
     new_weight = (weight.astype(jnp.float32) - step_size * full_delta.astype(jnp.float32)).astype(

time: 746 us -> 817 us (1.095)
  local copies, waits for them, and re-layouts: 72.4 us -> 129 us
  waiting for transfers between devices: 334 us -> 359 us
    unnamed x26 -> x93, local copies, waits for them, and re-layouts: 28.4 us -> 84.9 us
    all_to_all x1, waiting for transfers between devices: 0.01 us -> 23.4 us  [per_device(): lax.all_to_all(delta.reshape(capacity, owners, shard, quarter), 'rows', s...]
  transfers between devices with their start and end apart: 6 -> 6, of which waited for: 4 -> 5; matrix products, arithmetic and copies ran while one was open for 39% -> 9% of each run, Pallas kernels for 0% -> 0%
where the time goes in v1:
time: 817 us; the launch traced here: 810 us
  waiting for transfers between devices  359 us (44%)
  other arithmetic  220 us (27%)
  local copies, waits for them, and re-layouts  129 us (16%)
  matrix products  51.1 us (6%)
  starting transfers between devices  36.8 us (5%)
  between operations  14.6 us (2%)
    all_to_all x1, waiting for transfers between devices, per_device(): lax.all_to_all(spread_half(place_half, total, capacity, owners), 'rows',...  180 us
    another operation x10, other arithmetic, per_device(): lower = jnp.linalg.cholesky(gram)  134 us
    unnamed x93, local copies, waits for them, and re-layouts  84.9 us
    another operation x4, other arithmetic, per_device(): lax.linalg.triangular_solve(lower, sample, left_side=False, lower=True, t...  79.9 us
    psum x1, waiting for transfers between devices, per_device(): total = lax.psum(grads[0], 'dp').astype(jnp.float32).astype(jnp.bfloat16)  65.6 us
    all_to_all x1, waiting for transfers between devices, per_device(): lax.all_to_all(jnp.stack(jnp.split(new_basis.reshape(capacity, owners, sh...  53 us
    all_gather x1, waiting for transfers between devices, per_device(): lax.all_gather(collect_half(place_half, back_delta), 'dp', axis=2, tiled=...  36.3 us
    all_to_all x1, waiting for transfers between devices, per_device(): lax.all_to_all(delta.reshape(capacity, owners, shard, quarter), 'rows', s...  23.4 us
  transfers between devices with their start and end apart: 6, of which 5 were waited for; matrix products, arithmetic and copies ran while one was open for 9% of the time, Pallas kernels for 0%

profile of v1, /device:TPU:1, one launch (start us, length us, event | category | flops | bytes accessed | tf_op | source)
XLA Modules:
  0.0 810.5 jit_solution(14895756576859859116)
XLA Ops:
  8.8 3.5 fusion.5
  12.2 4.4 copy.201
  16.6 13.5 %all-to-all-start = ((f32[4,64,16,256]{3,2,0,1:T(8,128)}), f32[4,64,16,256]{3,2,0,1:T(8,128)}, u32[]{:S(2)}, u32[]{:S(2)}) async-start(f32[4,64,16,256]{3,2,0,1:T(8,128)} %copy.201), calls=%async_computation | async-start | bytes 8388608 | tf_op jit(solution)/shard_map/all_to_all | solution.py:63
  30.5 2.6 copy.234
  33.1 65.6 %all-reduce.3.cloned.1.call-done = bf16[64,16384]{1,0:T(8,128)(2,1)} async-done(((bf16[64,16384]{1,0:T(8,128)(2,1)}), bf16[64,16384]{1,0:T(8,128)(2,1)}) %all-reduce.3.cloned.1.call-update) | async-done | bytes 2097168 | tf_op jit(solution)/shard_map/psum | solution.py:71
  98.7 7.3 convolution_convert_fusion
  105.9 15.8 %copy.235 = bf16[32,8,16,1024]{3,2,1,0:T(8,128)(2,1)} copy(bf16[32,8,16,1024]{3,1,2,0:T(8,128)(2,1)} %bitcast.350) | data formatting | bytes 16777216
  121.7 8.5 %copy.203 = bf16[4,64,16,1024]{3,2,0,1:T(8,128)(2,1)} copy(bf16[4,64,16,1024]{3,2,1,0:T(8,128)(2,1)} %bitcast.351) | data formatting | bytes 16777216 | tf_op jit(solution)/shard_map/reshape | solution.py:25
  130.2 11.0 %all-to-all-start.1 = ((bf16[4,64,16,1024]{3,2,0,1:T(8,128)(2,1)}), bf16[4,64,16,1024]{3,2,0,1:T(8,128)(2,1)}, u32[]{:S(2)}, u32[]{:S(2)}) async-start(bf16[4,64,16,1024]{3,2,0,1:T(8,128)(2,1)} %copy.203), calls=%async_computation.1 | async-start | bytes 16777216 | tf_op jit(solution)/shard_map/all_to_all | solution.py:72
  141.9 4.7 copy.202
  146.6 180.4 %all-to-all-done.1 = bf16[4,64,16,1024]{3,2,0,1:T(8,128)(2,1)} async-done(((bf16[4,64,16,1024]{3,2,0,1:T(8,128)(2,1)}), bf16[4,64,16,1024]{3,2,0,1:T(8,128)(2,1)}, u32[]{:S(2)}, u32[]{:S(2)}) %all-to-all-start.1) | async-done | bytes 8388640 | tf_op jit(solution)/shard_map/all_to_all | solution.py:72
  327.0 8.5 %copy.204 = bf16[4,64,16,1024]{3,2,1,0:T(8,128)(2,1)} copy(bf16[4,64,16,1024]{3,2,0,1:T(8,128)(2,1)} %all-to-all-done.1) | data formatting | bytes 16777216 | tf_op jit(solution)/shard_map/all_to_all | solution.py:72
  335.6 5.8 fusion.14
  341.4 2.0 copy-done.2
  343.4 7.1 fusion.50
  352.1 47.1 %custom-call.16 = f32[4,128,128]{2,1,0:T(8,128)S(1)} custom-call(f32[4,128,128]{2,1,0:T(8,128)S(1)} %cholesky.122), custom_call_target="Cholesky" | custom-call | tf_op jit(solution)/shard_map/jit(cholesky)/cholesky | solution.py:103
  399.3 39.3 %custom-call.17 = f32[4,1,128,128]{2,3,1,0:T(8,128)S(1)} custom-call(f32[4,1,128,128]{3,2,1,0:T(8,128)S(1)} %select_bitcast_fusion), custom_call_target="InvertDiagBlocksLowerTriangular" | custom-call | tf_op jit(solution)/shard_map/jit(cholesky)/cholesky | solution.py:103
  440.0 1.6 convolution_subtract_fusion
  441.6 46.9 %custom-call.18 = f32[4,128,128]{2,1,0:T(8,128)S(1)} custom-call(f32[4,128,128]{2,1,0:T(8,128)S(1)} %convolution_subtract_fusion), custom_call_target="Cholesky" | custom-call | tf_op jit(solution)/shard_map/jit(cholesky)/cholesky | solution.py:103
  489.1 5.5 while.1
  489.7 2.1 bitcast_dynamic-update-slice_fusion.2
  492.4 2.1 bitcast_dynamic-update-slice_fusion.2
  494.5 79.6 %custom-call.19 = f32[4,2,128,128]{2,3,1,0:T(8,128)S(1)} custom-call(f32[4,2,128,128]{3,2,1,0:T(8,128)} %bitcast.369), custom_call_target="InvertDiagBlocksLowerTriangular" | custom-call | tf_op jit(solution)/shard_map/triangular_solve | solution.py:105
  574.2 3.7 fusion.1
  577.9 1.9 fusion.19
  579.8 2.0 fusion
  610.5 6.8 broadcast_multiply_fusion
  617.3 5.1 multiply_convert_fusion
  622.4 1.6 copy.206
  624.0 5.9 all-to-all-start.2
  629.9 1.5 constant_dynamic-update-slice_fusion.18
  631.4 1.5 constant_dynamic-update-slice_fusion.17
  637.3 1.5 constant_dynamic-update-slice_fusion.13
  646.0 1.5 constant_dynamic-update-slice_fusion.7
  647.5 1.5 constant_dynamic-update-slice_fusion.6
  650.4 1.5 constant_dynamic-update-slice_fusion.4
  651.9 1.5 constant_dynamic-update-slice_fusion.3
  656.3 1.5 constant_dynamic-update-slice_fusion
  657.8 23.4 %all-to-all-done.2 = bf16[4,64,16,256]{3,2,0,1:T(8,128)(2,1)S(1)} async-done(((bf16[4,64,16,256]{3,2,0,1:T(8,128)(2,1)}), bf16[4,64,16,256]{3,2,0,1:T(8,128)(2,1)S(1)}, u32[]{:S(2)}, u32[]{:S(2)}) %all-to-all-start.2) | async-done | bytes 2097184 | tf_op jit(solution)/shard_map/all_to_all | solution.py:108
  681.2 6.0 all-to-all-start.3
  689.9 36.3 %all-gather.2.cloned.1.call-done = bf16[64,16,1024]{2,1,0:T(8,128)(2,1)} async-done(((bf16[64,16,256]{2,1,0:T(8,128)(2,1)}), bf16[64,16,1024]{2,1,0:T(8,128)(2,1)}) %all-gather.2.cloned.1.call-update) | async-done | bytes 2097168 | tf_op jit(solution)/shard_map/all_gather | solution.py:115
  726.2 3.9 subtract_convert_fusion
  730.1 53.0 %all-to-all-done.3 = f32[64,4,1,16,256]{4,3,1,2,0:T(8,128)} async-done(((f32[64,4,1,16,256]{4,3,1,2,0:T(8,128)}), f32[64,4,1,16,256]{4,3,1,2,0:T(8,128)}, u32[]{:S(2)}, u32[]{:S(2)}) %all-to-all-start.3) | async-done | bytes 4194336 | tf_op jit(solution)/shard_map/all_to_all | solution.py:117
  783.1 2.8 copy.217
  785.9 5.7 copy.238
  791.6 5.8 copy.218
  797.4 4.5 fusion.31
  801.9 1.6 copy.219
  (120 shorter events, 54.6 us)
Async XLA Ops:
  7.2 328.4 %copy-start = (bf16[1024,256]{1,0:T(8,128)(2,1)S(1)}, bf16[1024,256]{1,0:T(8,128)(2,1)}, u32[]{:S(2)}) copy-start(bf16[1024,256]{1,0:T(8,128)(2,1)} %param.13) | copy-start | bytes 1572868
  16.6 13.9 %copy-start.8 = (bf16[1,64,16,1024]{3,2,1,0:T(8,128)(2,1)S(1)}, bf16[1,64,16,1024]{3,2,1,0:T(8,128)(2,1)}, u32[]{:S(2)}) copy-start(bf16[1,64,16,1024]{3,2,1,0:T(8,128)(2,1)} %param.8) | copy-start | bytes 6291460
  16.6 113.6 %all-to-all-start = ((f32[4,64,16,256]{3,2,0,1:T(8,128)}), f32[4,64,16,256]{3,2,0,1:T(8,128)}, u32[]{:S(2)}, u32[]{:S(2)}) async-start(f32[4,64,16,256]{3,2,0,1:T(8,128)} %copy.201), calls=%async_computation | async-start | bytes 8388608 | tf_op jit(solution)/shard_map/all_to_all | solution.py:63
  30.1 68.6 %all-reduce.3.cloned.1.call-start = ((), (), s32[]{:S(2)}) async-start(), calls=%async_computation.4 | async-start | bytes 4194304 | tf_op jit(solution)/shard_map/psum | solution.py:71
  130.2 11.3 %copy-start.11 = (s32[64]{0:T(128)S(1)}, s32[64]{0:T(128)}, u32[]{:S(2)}) copy-start(s32[64]{0:T(128)} %param.15) | copy-start | bytes 772
  130.2 196.8 %all-to-all-start.1 = ((bf16[4,64,16,1024]{3,2,0,1:T(8,128)(2,1)}), bf16[4,64,16,1024]{3,2,0,1:T(8,128)(2,1)}, u32[]{:S(2)}, u32[]{:S(2)}) async-start(bf16[4,64,16,1024]{3,2,0,1:T(8,128)(2,1)} %copy.203), calls=%async_computation.1 | async-start | bytes 16777216 | tf_op jit(solution)/shard_map/all_to_all | solution.py:72
  341.4 2.0 copy-start.2
  351.1 1.0 copy-start.6
  574.2 5.6 copy-start.3
  581.8 28.6 %copy-start.10 = (f32[4,256,256]{2,1,0:T(8,128)S(1)}, f32[4,256,256]{2,1,0:T(8,128)}, u32[]{:S(2)}) copy-start(f32[4,256,256]{2,1,0:T(8,128)} %param.11) | copy-start | bytes 3145732
  582.3 35.0 %copy-start.5 = (f32[4,64,16,256]{3,2,0,1:T(8,128)}, f32[4,64,16,256]{3,2,0,1:T(8,128)S(1)}, u32[]{:S(2)}) copy-start(f32[4,64,16,256]{3,2,0,1:T(8,128)S(1)} %copy_multiply_fusion) | copy-start | bytes 12582916
  582.3 28.1 %copy-start.4 = (f32[4,64,16,256]{3,2,1,0:T(8,128)S(1)}, f32[4,64,16,256]{3,2,1,0:T(8,128)}, u32[]{:S(2)}) copy-start(f32[4,64,16,256]{3,2,1,0:T(8,128)} %copy.202) | copy-start | bytes 12582916
  582.3 28.1 %copy-start.9 = (f32[4,256,256]{2,1,0:T(8,128)S(1)}, f32[4,256,256]{2,1,0:T(8,128)}, u32[]{:S(2)}) copy-start(f32[4,256,256]{2,1,0:T(8,128)} %param.12) | copy-start | bytes 3145732
  624.0 57.2 %all-to-all-start.2 = ((bf16[4,64,16,256]{3,2,0,1:T(8,128)(2,1)}), bf16[4,64,16,256]{3,2,0,1:T(8,128)(2,1)S(1)}, u32[]{:S(2)}, u32[]{:S(2)}) async-start(bf16[4,64,16,256]{3,2,0,1:T(8,128)(2,1)} %copy.206), calls=%async_computation.2 | async-start | bytes 4194304 | tf_op jit(solution)/shard_map/all_to_all | solution.py:108
  681.2 101.9 %all-to-all-start.3 = ((f32[64,4,1,16,256]{4,3,1,2,0:T(8,128)}), f32[64,4,1,16,256]{4,3,1,2,0:T(8,128)}, u32[]{:S(2)}, u32[]{:S(2)}) async-start(f32[64,4,1,16,256]{4,3,1,2,0:T(8,128)} %constant_dynamic-update-slice_fusion), calls=%async_computation.3 | async-start | bytes 8388608 | tf_op jit(solution)/shard_map/all_to_all | solution.py:117
  687.2 39.0 %all-gather.2.cloned.1.call-start = ((), (), s32[]{:S(2)}) async-start(), calls=%async_computation.5 | async-start | bytes 2621440 | tf_op jit(solution)/shard_map/all_gather | solution.py:115
  687.5 38.8 %copy-start.7 = (bf16[64,16,1024]{2,1,0:T(8,128)(2,1)S(1)}, bf16[64,16,1024]{2,1,0:T(8,128)(2,1)}, u32[]{:S(2)}) copy-start(bf16[64,16,1024]{2,1,0:T(8,128)(2,1)} %param.9) | copy-start | bytes 6291460
  791.6 11.8 %copy-start.1 = (bf16[1024,256]{1,0:T(8,128)(2,1)S(1)}, bf16[1024,256]{1,0:T(8,128)(2,1)}, u32[]{:S(2)}) copy-start(bf16[1024,256]{1,0:T(8,128)(2,1)} %param.13) | copy-start | bytes 1572868
Sparse Core Ops, SparseCore 0:
  33.9 64.7 all-reduce.2
  690.6 35.6 all-gather.1
